TPU v7x, 32 devices: a whole 2x2x4 slice. The times are simulated.
32 devices in a mesh: cuts: 2 (over y), wide: 8 (over z, x), narrow: 2 (over core).
Axes of the slice: x: 2, y: 2, z: 4, core: 2. Of those that a mesh axis runs over, the one named last changes fastest.
Arguments:
- stem_tensor: float32 [2, 4194304], P(None, ('cuts', 'wide', 'narrow')), parts along dimension 1, may hold values from -6 to 6
- sub_branches: bfloat16 [3, 2, 2, 512, 512], P(None, 'narrow', None, 'wide'), may hold values from -0.1875 to 0.1875
- branch_bits: int32 [3, 9], replicated, may hold values from 7 to 20, as said below
Outputs:
- amplitudes: float32 [2, 4194304], P(None, ('cuts', 'wide', 'narrow')), parts along dimension 1
There are 2 independent parts, one for each index of `cuts`. A program takes and returns all parts, laid end to end along the dimension named above; an argument that names none is the same for every part. Nothing has to cross between parts.
Inputs may be any that keep to these rules, and one draw needn't show every extreme that they name: `branch_bits`: no bit below 7 is ever named. Row 0 holds 9 distinct bits of 7 to 16, bit 7 among them. Row 1 holds the 3 bits 17 + 1 to 20 and 6 distinct bits of 7 to 12. Row 2 holds bit 17 and 8 distinct bits of 7 to 12 and 18 to 20. Each row in any order.
All inputs are finite; a program needn't handle non-finite values.
Results may differ from a plain program's by a relative error of at most 0.005.
Values may be sent and summed in bfloat16 or wider, within the bound.
A program may use at most 64 MiB of HBM per device.

v0:
```python
import jax
import jax.numpy as jnp
from jax import lax
from jax.sharding import PartitionSpec as P

LBITS = 17
BBITS = 9
BRANCHES = 3


lane_bits = 7


def partner(value, axis, stride):
    mask = 2**stride
    pairs = [(source, source ^ mask) for source in range(lax.axis_size(axis))]
    return lax.ppermute(value, axis, pairs)


def bit_tables(chosen_bits, total_bits, width_bits):
    places = jnp.arange(total_bits, dtype=jnp.int32)
    orders = jnp.arange(width_bits, dtype=jnp.int32)
    matches = places[:, None] == chosen_bits[None, :]
    chosen = jnp.any(matches, axis=1)
    ranking = jnp.sum(jnp.where(matches, orders[None, :], 0), axis=1)
    unchosen = 1 - chosen.astype(jnp.int32)
    free_rank = jnp.cumsum(unchosen) - unchosen
    unit_ones = jnp.ones((total_bits,), jnp.int32)
    weight = jnp.where(
        chosen,
        jnp.left_shift(unit_ones, width_bits - 1 - ranking),
        jnp.left_shift(unit_ones, width_bits + free_rank),
    )
    low_bits = total_bits // 2

    def partial_table(count, first_place, last_place):
        values = jnp.arange(count, dtype=jnp.int32)
        running = jnp.zeros((count,), jnp.int32)
        for position in range(first_place, last_place):
            running = (
                running
                + jnp.bitwise_and(jnp.right_shift(values, position - first_place), 1)
                * weight[position]
            )
        return running

    inverse = (
        partial_table(2 ** (total_bits - low_bits), low_bits, total_bits)[:, None]
        + partial_table(2**low_bits, 0, low_bits)[None, :]
    ).reshape(-1)
    columns = jnp.arange(2**width_bits, dtype=jnp.int32)
    col_part = jnp.zeros((2**width_bits,), jnp.int32)
    for slot_no in range(width_bits):
        col_part = col_part + jnp.left_shift(
            jnp.bitwise_and(jnp.right_shift(columns, width_bits - 1 - slot_no), 1),
            chosen_bits[slot_no],
        )
    row_ids = jnp.arange(2 ** (total_bits - width_bits), dtype=jnp.int32)
    row_part = jnp.zeros((2 ** (total_bits - width_bits),), jnp.int32)
    for position in range(total_bits):
        bit_value = jnp.bitwise_and(jnp.right_shift(row_ids, free_rank[position]), 1) * 2**position
        row_part = row_part + jnp.where(chosen[position], 0, bit_value)
    gather_index = row_part[:, None] + col_part[None, :]
    return (gather_index, inverse)


def half_product(first_matrix, second_matrix):
    return jnp.dot(first_matrix, second_matrix, preferred_element_type=jnp.float32)


def merge_branch(left_factor, right_factor):
    real_part = half_product(left_factor[0], right_factor[0]) - half_product(
        left_factor[1], right_factor[1]
    )
    imag_part = half_product(left_factor[0], right_factor[1]) + half_product(
        left_factor[1], right_factor[0]
    )
    return jnp.stack([real_part, imag_part]).astype(jnp.bfloat16)


def contract_blocks(amplitude, branch, gather_index, inverse):
    lanes = 2**lane_bits
    blocks = amplitude.reshape(2, -1, lanes)
    picked = jnp.take(blocks, gather_index, axis=1)
    widened = branch.astype(jnp.float32)

    def real_product(data, matrix):
        return jnp.einsum(
            "rul,cu->rcl",
            data,
            matrix,
            precision=lax.Precision.HIGHEST,
            preferred_element_type=jnp.float32,
        )

    real_part = real_product(picked[0], widened[0]) - real_product(picked[1], widened[1])
    imag_part = real_product(picked[0], widened[1]) + real_product(picked[1], widened[0])
    merged = jnp.stack([real_part, imag_part]).reshape(2, -1, lanes)
    return jnp.take(merged, inverse, axis=1).reshape(2, -1)


def shards(stem_tensor, sub_branches, branch_bits):
    wide_count = lax.axis_size("wide")
    wide_log = wide_count.bit_length() - 1
    local_bits = LBITS
    block_shape = (2, wide_count, 2, stem_tensor.shape[1] // (2 * wide_count))
    leading = lax.axis_index("narrow") == 0

    def move_wide(amplitude):
        return lax.all_to_all(
            amplitude.reshape(block_shape), "wide", split_axis=1, concat_axis=1, tiled=True
        ).reshape(2, -1)

    def move_narrow(amplitude):
        return lax.all_to_all(
            amplitude.reshape(block_shape), "narrow", split_axis=2, concat_axis=2, tiled=True
        ).reshape(2, -1)

    def working_places(which):
        chosen_bits = branch_bits[which]
        if which == 0:
            return chosen_bits - lane_bits
        shifted = jnp.where(chosen_bits == local_bits, local_bits - wide_log - 1, chosen_bits)
        placed = jnp.where(chosen_bits > local_bits, chosen_bits - wide_log - 1, shifted)
        return placed - lane_bits

    amplitude = stem_tensor
    for which in range(BRANCHES):
        own_rows = sub_branches[which, 0]
        own_whole = lax.all_gather(own_rows, "wide", axis=1, tiled=True)
        partner_whole = partner(own_whole, "narrow", 0)
        branch = merge_branch(
            jnp.where(leading, own_whole, partner_whole),
            jnp.where(leading, partner_whole, own_whole),
        )
        if which == 1:
            amplitude = move_wide(amplitude)
        if which == 2:
            amplitude = move_narrow(amplitude)
        gather_index, inverse = bit_tables(working_places(which), local_bits - lane_bits, BBITS)
        amplitude = contract_blocks(amplitude, branch, gather_index, inverse)
    amplitude = move_narrow(amplitude)
    amplitude = move_wide(amplitude)
    return amplitude


def solution(mesh):
    in_specs = (P(None, ("cuts", "wide", "narrow")), P(None, "narrow", None, "wide", None), P())
    out_specs = P(None, ("cuts", "wide", "narrow"))
    return jax.shard_map(shards, mesh=mesh, in_specs=in_specs, out_specs=out_specs, check_vma=False)
```

profile of v0, /device:TPU:0, one launch (start us, length us, event | category | flops | bytes accessed | tf_op | source)
XLA Modules:
  0.0 283.8 jit_solution(12411207935728170080)
XLA Ops:
  12.4 5.5 %shift-left_add_fusion.2 = s32[512]{0:T(512)S(1)} fusion(s32[]{:T(128)} %bitcast.145, s32[]{:T(128)} %bitcast.144, s32[]{:T(128)} %bitcast.143, s32[]{:T(128)} %bitcast.142, s32[]{:T(128)} %bitcast.141, s32[]{:T(128)} %bitcast.140, s32[]{:T(128)} %bitcast.139, s32[]{:T(128)} %bitcast.138, s32[]{:T(128)} %bitcast.137), kind=kLoop, calls=%fused_computation.114 | loop fusion | flops 17920 | bytes 2084 | tf_op jit(solution)/shard_map/add | solution.py:54
  17.9 12.4 %fusion.41 = s32[2]{0:T(128)S(1)} fusion(pred[]{:T(512)} %bitcast.131, pred[]{:T(512)} %bitcast.133, pred[]{:T(512)} %bitcast.135, pred[]{:T(512)} %bitcast.129, pred[]{:T(512)} %bitcast.127, pred[]{:T(512)} %bitcast.125, pred[]{:T(512)} %bitcast.123, pred[]{:T(512)} %bitcast.121, pred[]{:T(512)} %bitcast.119, pred[]{:T(512)} %bitcast.117, s32[]{:T(128)} %bitcast.136, ...), kind=kLoop, calls=%fused_computation.166 | loop fusion | flops 96 | bytes 58 | tf_op jit(solution)/shard_map/add | solution.py:62
  31.2 6.2 %multiply_add_fusion.4 = (s32[32]{0:T(128)S(1)}, s32[32]{0:T(128)S(1)}) fusion(s32[]{:T(128)} %bitcast.110, s32[]{:T(128)} %bitcast.109, s32[]{:T(128)} %bitcast.108, s32[]{:T(128)} %bitcast.107, s32[]{:T(128)} %bitcast.106, s32[]{:T(128)} %bitcast.105, s32[]{:T(128)} %bitcast.104, s32[]{:T(128)} %bitcast.103, s32[]{:T(128)} %bitcast.102, s32[]{:T(128)} %bitcast.101), kind=kLoop, calls=%fused_computation.204 | loop fusion | flops 896 | bytes 296 | tf_op jit(solution)/shard_map/add | solution.py:41
  40.7 3.1 %multiply_add_fusion.2 = s32[32]{0:T(128)S(1)} fusion(s32[]{:T(128)} %bitcast.61, s32[]{:T(128)} %bitcast.60, s32[]{:T(128)} %bitcast.59, s32[]{:T(128)} %bitcast.58, s32[]{:T(128)} %bitcast.57), kind=kLoop, calls=%fused_computation.199 | loop fusion | flops 608 | bytes 148 | tf_op jit(solution)/shard_map/add | solution.py:41
  43.8 3.1 %multiply_add_fusion.3 = s32[32]{0:T(128)S(1)} fusion(s32[]{:T(128)} %bitcast.56, s32[]{:T(128)} %bitcast.55, s32[]{:T(128)} %bitcast.54, s32[]{:T(128)} %bitcast.53, s32[]{:T(128)} %bitcast.52), kind=kLoop, calls=%fused_computation.200 | loop fusion | flops 608 | bytes 148 | tf_op jit(solution)/shard_map/add | solution.py:41
  55.8 5.7 %shift-left_add_fusion.1 = s32[512]{0:T(512)S(1)} fusion(s32[]{:T(128)} %bitcast.97, s32[]{:T(128)} %bitcast.96, s32[]{:T(128)} %bitcast.95, s32[]{:T(128)} %bitcast.94, s32[]{:T(128)} %bitcast.93, s32[]{:T(128)} %bitcast.92, s32[]{:T(128)} %bitcast.91, s32[]{:T(128)} %bitcast.90, s32[]{:T(128)} %bitcast.89), kind=kLoop, calls=%fused_computation.113 | loop fusion | flops 17920 | bytes 2084 | tf_op jit(solution)/shard_map/add | solution.py:54
  61.5 12.4 %fusion.50 = s32[2]{0:T(128)S(1)} fusion(pred[]{:T(512)} %bitcast.82, pred[]{:T(512)} %bitcast.84, pred[]{:T(512)} %bitcast.86, pred[]{:T(512)} %bitcast.80, pred[]{:T(512)} %bitcast.78, pred[]{:T(512)} %bitcast.76, pred[]{:T(512)} %bitcast.74, pred[]{:T(512)} %bitcast.72, pred[]{:T(512)} %bitcast.70, pred[]{:T(512)} %bitcast.68, s32[]{:T(128)} %bitcast.87, ...), kind=kLoop, calls=%fused_computation.175 | loop fusion | flops 96 | bytes 58 | tf_op jit(solution)/shard_map/add | solution.py:62
  73.9 5.6 %shift-left_add_fusion = s32[512]{0:T(512)S(1)} fusion(s32[]{:T(128)} %bitcast.48, s32[]{:T(128)} %bitcast.47, s32[]{:T(128)} %bitcast.46, s32[]{:T(128)} %bitcast.45, s32[]{:T(128)} %bitcast.44, s32[]{:T(128)} %bitcast.43, s32[]{:T(128)} %bitcast.42, s32[]{:T(128)} %bitcast.41, s32[]{:T(128)} %bitcast.40), kind=kLoop, calls=%fused_computation.112 | loop fusion | flops 17920 | bytes 2084 | tf_op jit(solution)/shard_map/add | solution.py:54
  79.6 12.4 %fusion.59 = s32[2]{0:T(128)S(1)} fusion(pred[]{:T(512)} %bitcast.33, pred[]{:T(512)} %bitcast.35, pred[]{:T(512)} %bitcast.37, pred[]{:T(512)} %bitcast.31, pred[]{:T(512)} %bitcast.29, pred[]{:T(512)} %bitcast.27, pred[]{:T(512)} %bitcast.25, pred[]{:T(512)} %bitcast.23, pred[]{:T(512)} %bitcast.21, pred[]{:T(512)} %bitcast.19, s32[]{:T(128)} %bitcast.38, ...), kind=kLoop, calls=%fused_computation.184 | loop fusion | flops 96 | bytes 58 | tf_op jit(solution)/shard_map/add | solution.py:62
  93.9 3.5 %gather_fusion = f32[1024,2,128]{2,1,0:T(2,128)S(1)} fusion(f32[2,1024,128]{2,0,1:T(2,128)S(1)} %bitcast.311, s32[1024]{0:T(1024)S(1)} %broadcast_clamp_fusion.2), kind=kCustom, calls=%fused_computation.clone | custom fusion | bytes 2101248 | tf_op jit(solution)/shard_map/jit(_take)/gather | solution.py:84
  97.8 37.2 %all-gather.7.cloned.1.call-done = bf16[1,1,2,512,512]{4,3,2,1,0:T(8,128)(2,1)} async-done(((bf16[1,1,2,64,512]{4,3,2,1,0:T(8,128)(2,1)}), bf16[1,1,2,512,512]{4,3,2,1,0:T(8,128)(2,1)}) %all-gather.7.cloned.1.call-update) | async-done | bytes 1048592 | tf_op jit(solution)/shard_map/all_gather | solution.py:130
  142.8 7.6 %gather_fusion.1 = f32[1024,2,128]{2,1,0:T(2,128)} fusion(f32[2,1024,128]{2,0,1:T(2,128)S(1)} %pad_maximum_fusion, s32[1024]{0:T(1024)S(1)} %fusion.27), kind=kCustom, calls=%fused_computation.1.clone | custom fusion | bytes 2101248 | tf_op jit(solution)/shard_map/jit(_take)/gather | solution.py:99
  150.3 5.3 %select_bitcast_fusion.4 = f32[2,1024,128]{2,0,1:T(2,128)S(1)} fusion(f32[1024,2,128]{2,1,0:T(2,128)} %gather_fusion.1, pred[1024]{0:T(1024)(128)(4,1)S(1)} %compare_and_fusion.5), kind=kLoop, calls=%fused_computation.37 | loop fusion | flops 262144 | bytes 2098176 | tf_op jit(solution)/shard_map/jit(_take)/select_n | solution.py:99
  159.6 4.4 %all-to-all-start = ((f32[2,8,2,8192]{3,2,0,1:T(2,128)}), f32[2,8,2,8192]{3,2,0,1:T(2,128)}, u32[]{:S(2)}, u32[]{:S(2)}) async-start(f32[2,8,2,8192]{3,2,0,1:T(2,128)} %copy.72), calls=%async_computation | async-start | bytes 2097152 | tf_op jit(solution)/shard_map/all_to_all | solution.py:110
  169.7 20.9 %all-to-all-done = f32[2,8,2,8192]{3,2,0,1:T(2,128)} async-done(((f32[2,8,2,8192]{3,2,0,1:T(2,128)}), f32[2,8,2,8192]{3,2,0,1:T(2,128)}, u32[]{:S(2)}, u32[]{:S(2)}) %all-to-all-start) | async-done | bytes 1048608 | tf_op jit(solution)/shard_map/all_to_all | solution.py:110
  195.7 7.5 %gather_fusion.2 = f32[1024,2,128]{2,1,0:T(2,128)} fusion(f32[2,1024,128]{2,0,1:T(2,128)S(1)} %copy.74, s32[1024]{0:T(1024)S(1)} %broadcast_clamp_fusion.1), kind=kCustom, calls=%fused_computation.2.clone | custom fusion | bytes 2101248 | tf_op jit(solution)/shard_map/jit(_take)/gather | solution.py:84
  208.3 3.5 %gather_fusion.3 = f32[1024,2,128]{2,1,0:T(2,128)S(1)} fusion(f32[2,1024,128]{2,0,1:T(2,128)S(1)} %pad_maximum_fusion.1, s32[1024]{0:T(1024)S(1)} %fusion.28), kind=kCustom, calls=%fused_computation.4.clone | custom fusion | bytes 2101248 | tf_op jit(solution)/shard_map/jit(_take)/gather | solution.py:99
  211.9 3.7 %select_bitcast_fusion.2 = f32[2,1024,128]{2,0,1:T(2,128)S(1)} fusion(f32[1024,2,128]{2,1,0:T(2,128)S(1)} %gather_fusion.3, pred[1024]{0:T(1024)(128)(4,1)S(1)} %compare_and_fusion.4), kind=kLoop, calls=%fused_computation.35 | loop fusion | flops 262144 | bytes 2098176 | tf_op jit(solution)/shard_map/jit(_take)/select_n | solution.py:99
  216.9 4.6 %all_to_all.20 = f32[2,8,2,8192]{3,1,0,2:T(8,128)S(1)} all-to-all(f32[2,8,2,8192]{3,1,0,2:T(8,128)S(1)} %copy.79), channel_id=1, replica_groups=mesh['cuts'=2,'wide'=8,'narrow'=2] {'narrow'}, dimensions={2} | all-to-all | bytes 2097152 | tf_op jit(solution)/shard_map/all_to_all | solution.py:115
  224.0 3.6 %gather_fusion.4 = f32[1024,2,128]{2,1,0:T(2,128)S(1)} fusion(f32[2,1024,128]{2,0,1:T(2,128)S(1)} %copy.81, s32[1024]{0:T(1024)S(1)} %broadcast_clamp_fusion), kind=kCustom, calls=%fused_computation.3.clone | custom fusion | bytes 2101248 | tf_op jit(solution)/shard_map/jit(_take)/gather | solution.py:84
  231.5 3.6 %gather_fusion.5 = f32[1024,2,128]{2,1,0:T(2,128)S(1)} fusion(f32[2,1024,128]{2,0,1:T(2,128)S(1)} %pad_maximum_fusion.2, s32[1024]{0:T(1024)S(1)} %fusion.29), kind=kCustom, calls=%fused_computation.5.clone | custom fusion | bytes 2101248 | tf_op jit(solution)/shard_map/jit(_take)/gather | solution.py:99
  235.0 3.7 %select_bitcast_fusion = f32[2,1024,128]{2,0,1:T(2,128)S(1)} fusion(f32[1024,2,128]{2,1,0:T(2,128)S(1)} %gather_fusion.5, pred[1024]{0:T(1024)(128)(4,1)S(1)} %compare_and_fusion.3), kind=kLoop, calls=%fused_computation.33 | loop fusion | flops 262144 | bytes 2098176 | tf_op jit(solution)/shard_map/jit(_take)/select_n | solution.py:99
  240.1 4.6 %all_to_all.21 = f32[2,8,2,8192]{3,1,0,2:T(8,128)S(1)} all-to-all(f32[2,8,2,8192]{3,1,0,2:T(8,128)S(1)} %copy.86), channel_id=1, replica_groups=mesh['cuts'=2,'wide'=8,'narrow'=2] {'narrow'}, dimensions={2} | all-to-all | bytes 2097152 | tf_op jit(solution)/shard_map/all_to_all | solution.py:115
  245.5 29.4 %all_to_all.22 = f32[2,8,2,8192]{3,2,0,1:T(2,128)S(1)} all-to-all(f32[2,8,2,8192]{3,2,0,1:T(2,128)S(1)} %copy.87), channel_id=1, replica_groups=mesh['cuts'=2,'wide'=8,'narrow'=2] {'wide'}, dimensions={1} | all-to-all | bytes 2097152 | tf_op jit(solution)/shard_map/all_to_all | solution.py:110
  (128 shorter events, 60.5 us)
Async XLA Ops:
  6.5 87.3 %copy-start = (f32[2,131072]{1,0:T(2,128)S(1)}, f32[2,131072]{1,0:T(2,128)}, u32[]{:S(2)}) copy-start(f32[2,131072]{1,0:T(2,128)} %param.7) | copy-start | bytes 3145732
  6.5 85.6 %all-gather.9.cloned.1.call-start = ((), (), s32[]{:S(2)}) async-start(), calls=%async_computation.5 | async-start | bytes 1179648 | tf_op jit(solution)/shard_map/all_gather | solution.py:130
  8.4 85.4 %all-gather.11.cloned.1.call-start = ((), (), s32[]{:S(2)}) async-start(), calls=%async_computation.6 | async-start | bytes 1179648 | tf_op jit(solution)/shard_map/all_gather | solution.py:130
  9.2 125.8 %all-gather.7.cloned.1.call-start = ((), (), s32[]{:S(2)}) async-start(), calls=%async_computation.4 | async-start | bytes 1179648 | tf_op jit(solution)/shard_map/all_gather | solution.py:130
  9.2 0.7 copy-start.3
  92.2 42.8 %collective-permute-start.1 = (bf16[2,512,512]{2,1,0:T(8,128)(2,1)}, bf16[2,512,512]{2,1,0:T(8,128)(2,1)}, u32[]{:S(2)}, u32[]{:S(2)}) collective-permute-start(bf16[2,512,512]{2,1,0:T(8,128)(2,1)} %bitcast.322), channel_id=1, source_target_pairs={{0,1},{1,0},{2,3},{3,2},{4,5},{5,4},{6,7},{7,6},{8,9},{9,8},{10,11... | collective-permute-start | bytes 3145736 | tf_op jit(solution)/shard_map/ppermute | solution.py:17
  93.8 41.2 %collective-permute-start.2 = (bf16[2,512,512]{2,1,0:T(8,128)(2,1)}, bf16[2,512,512]{2,1,0:T(8,128)(2,1)}, u32[]{:S(2)}, u32[]{:S(2)}) collective-permute-start(bf16[2,512,512]{2,1,0:T(8,128)(2,1)} %bitcast.323), channel_id=1, source_target_pairs={{0,1},{1,0},{2,3},{3,2},{4,5},{5,4},{6,7},{7,6},{8,9},{9,8},{10,11... | collective-permute-start | bytes 3145736 | tf_op jit(solution)/shard_map/ppermute | solution.py:17
  134.9 30.8 %collective-permute-start = (bf16[2,512,512]{2,1,0:T(8,128)(2,1)}, bf16[2,512,512]{2,1,0:T(8,128)(2,1)}, u32[]{:S(2)}, u32[]{:S(2)}) collective-permute-start(bf16[2,512,512]{2,1,0:T(8,128)(2,1)} %bitcast.321), channel_id=1, source_target_pairs={{0,1},{1,0},{2,3},{3,2},{4,5},{5,4},{6,7},{7,6},{8,9},{9,8},{10,11... | collective-permute-start | bytes 3145736 | tf_op jit(solution)/shard_map/ppermute | solution.py:17
  159.6 31.0 %all-to-all-start = ((f32[2,8,2,8192]{3,2,0,1:T(2,128)}), f32[2,8,2,8192]{3,2,0,1:T(2,128)}, u32[]{:S(2)}, u32[]{:S(2)}) async-start(f32[2,8,2,8192]{3,2,0,1:T(2,128)} %copy.72), calls=%async_computation | async-start | bytes 2097152 | tf_op jit(solution)/shard_map/all_to_all | solution.py:110
  165.3 1.2 copy-start.2
  274.9 2.3 copy-start.1
Sparse Core Ops, SparseCore 0:
  9.5 43.0 all-gather.8
  54.8 38.9 all-gather.10
  96.0 38.9 all-gather.6
where the time goes:
time: 285 us; the launch traced here: 284 us
  other arithmetic  94.5 us (33%)
  waiting for transfers between devices  60.5 us (21%)
  local copies, waits for them, and re-layouts  58.5 us (21%)
  blocking collectives  38.6 us (14%)
  between operations  13.7 us (5%)
  matrix products  13 us (5%)
  starting transfers between devices  5.07 us (2%)
    all_gather x3, waiting for transfers between devices, shards(): own_whole = lax.all_gather(own_rows, 'wide', axis=1, tiled=True)  38.2 us
    add x3, other arithmetic, bit_tables(): row_part = row_part + jnp.where(chosen[position], 0, bit_value)  37.2 us
    all_to_all x1, blocking collectives, move_wide(): lax.all_to_all(amplitude.reshape(block_shape), 'wide', split_axis=1, conc...  29.4 us
    all_to_all x1, waiting for transfers between devices, move_wide(): lax.all_to_all(amplitude.reshape(block_shape), 'wide', split_axis=1, conc...  20.9 us
    add x5, other arithmetic, partial_table(): running + jnp.bitwise_and(jnp.right_shift(values, position - first_place)...  18.6 us
    add x3, other arithmetic, bit_tables(): col_part + jnp.left_shift(jnp.bitwise_and(jnp.right_shift(columns, width_...  16.9 us
    gather x6, local copies, waits for them, and re-layouts, contract_blocks(): picked = jnp.take(blocks, gather_index, axis=1)  16.1 us
    gather x3, local copies, waits for them, and re-layouts, contract_blocks(): return jnp.take(merged, inverse, axis=1).reshape(2, -1)  14.7 us
  transfers between devices with their start and end apart: 7, of which 3 were waited for; matrix products, arithmetic and copies ran while one was open for 41% of the time, Pallas kernels for 0%

commit v1 on v0

--- a/solution.py
+++ b/solution.py
@@ -1,6 +1,10 @@
+import functools
+
 import jax
 import jax.numpy as jnp
 from jax import lax
+from jax.experimental import pallas as pl
+from jax.experimental.pallas import tpu as pltpu
 from jax.sharding import PartitionSpec as P
 
 LBITS = 17
@@ -144,7 +148,280 @@
     return amplitude
 
 
+MESH = pl.DeviceIdType.MESH
+
+
+def ring_place(wide, count):
+    return wide // 2 + (wide % 2) * (count - 1 - 2 * (wide // 2))
+
+
+def ring_member(place, count):
+    back = place // (count // 2)
+    return 2 * place + back * (2 * (count - 1 - place) + 1 - 2 * place)
+
+
+def stem_kernel(
+    count, places_ref, stem_ref, sub_ref, out_ref,
+    gath, bcat, work, prod, send, recv,
+    own_sem, ring_send, ring_recv, pair_send, pair_recv, swap_send, swap_recv,
+):
+    wide = lax.axis_index("wide")
+    narrow = lax.axis_index("narrow")
+    rows = sub_ref.shape[2]
+    branches = sub_ref.shape[0]
+    dim = bcat.shape[0]
+    total = stem_ref.shape[0]
+    bits = total.bit_length() - 1
+    half = count // 2
+    lanes = stem_ref.shape[1] // 2
+    place = ring_place(wide, count)
+    neighbours = (
+        ring_member((place + 1) % count, count),
+        ring_member((place + count - 1) % count, count),
+    )
+    members = 2 * count
+    me = wide * 2 + narrow
+    piece = total // members
+
+    barrier = pltpu.get_barrier_semaphore()
+    for neighbour in neighbours:
+        pl.semaphore_signal(barrier, inc=1, device_id={"wide": neighbour}, device_id_type=MESH)
+    pl.semaphore_signal(barrier, inc=1, device_id={"narrow": 1 - narrow}, device_id_type=MESH)
+    pl.semaphore_wait(barrier, 3)
+
+    def block_rows(offset):
+        origin = ring_member((place + count - offset) % count, count)
+        return pl.ds(pl.multiple_of(origin * rows, rows), rows)
+
+    def used(way, part, distance):
+        return distance < half or (distance == half and part == way)
+
+    def offset_of(way, distance):
+        return distance if way == 0 else (count - distance) % count
+
+    started = []
+
+    def ring_copy(way, which, part, distance):
+        target = gath.at[narrow, which, part, block_rows(offset_of(way, distance - 1))]
+        return pltpu.make_async_remote_copy(
+            src_ref=sub_ref.at[which, part] if distance == 1 else target,
+            dst_ref=target,
+            send_sem=ring_send.at[way, which, part, distance - 1],
+            recv_sem=ring_recv.at[way, which, part, distance - 1],
+            device_id={"wide": neighbours[way]},
+            device_id_type=MESH,
+        )
+
+    def pair_copy(which, part, offset):
+        target = gath.at[narrow, which, part, block_rows(offset)]
+        return pltpu.make_async_remote_copy(
+            src_ref=sub_ref.at[which, part] if offset == 0 else target,
+            dst_ref=target,
+            send_sem=pair_send.at[which, part, offset],
+            recv_sem=pair_recv.at[which, part, offset],
+            device_id={"narrow": 1 - narrow},
+            device_id_type=MESH,
+        )
+
+    def launch(copy):
+        copy.start()
+        started.append(copy)
+
+    own_copies = []
+
+    def send_own(which):
+        for part in range(2):
+            for way in range(2):
+                if used(way, part, 1):
+                    launch(ring_copy(way, which, part, 1))
+        for part in range(2):
+            launch(pair_copy(which, part, 0))
+            keep = pltpu.make_async_copy(
+                sub_ref.at[which, part],
+                gath.at[narrow, which, part, block_rows(0)],
+                own_sem.at[which, part],
+            )
+            keep.start()
+            own_copies.append(keep)
+
+    def relay(which):
+        for distance in range(1, half + 1):
+            for part in range(2):
+                for way in range(2):
+                    if not used(way, part, distance):
+                        continue
+                    ring_copy(way, which, part, distance).wait_recv()
+                    if used(way, part, distance + 1):
+                        launch(ring_copy(way, which, part, distance + 1))
+                    launch(pair_copy(which, part, offset_of(way, distance)))
+            if distance == max(half - 1, 1) and which + 1 < branches:
+                send_own(which + 1)
+        for part in range(2):
+            own_copies[2 * which + part].wait()
+            for offset in range(count):
+                pair_copy(which, part, offset).wait_recv()
+
+    def merge(which):
+        first = [gath[0, which, part] for part in range(2)]
+        second = [gath[1, which, part] for part in range(2)]
+
+        def half_product(left, right):
+            return jnp.dot(left, right, preferred_element_type=jnp.float32)
+
+        bcat[:, :dim] = (
+            half_product(first[0], second[0]) - half_product(first[1], second[1])
+        ).astype(jnp.bfloat16)
+        bcat[:, dim:] = (
+            half_product(first[0], second[1]) + half_product(first[1], second[0])
+        ).astype(jnp.bfloat16)
+
+    width = dim.bit_length() - 1
+
+    def free_place(which):
+        rest = bits * (bits - 1) // 2
+        for slot in range(width):
+            rest = rest - places_ref[which, slot]
+        return rest
+
+    def bit_at(values, position):
+        return jnp.bitwise_and(jnp.right_shift(values, position), 1)
+
+    def gathered_place(which, values):
+        found = jnp.left_shift(bit_at(values, free_place(which)), width)
+        for slot in range(width):
+            found = found + jnp.left_shift(
+                bit_at(values, places_ref[which, slot]), width - 1 - slot
+            )
+        return found
+
+    def natural_place(which, values):
+        found = jnp.left_shift(bit_at(values, width), free_place(which))
+        for slot in range(width):
+            found = found + jnp.left_shift(
+                bit_at(values, width - 1 - slot), places_ref[which, slot]
+            )
+        return found
+
+    def permute(source, target_ref, goal):
+        step = min(256, total)
+        for first in range(0, total, step):
+            index = lax.broadcasted_iota(jnp.int32, (step, total), 0) + first
+            onehot = (index == goal).astype(jnp.float32).astype(jnp.bfloat16)
+            target_ref[first:first + step, :] = jnp.dot(
+                onehot, source, preferred_element_type=jnp.float32
+            ).astype(jnp.bfloat16)
+
+    def contract():
+        for first in range(0, total, dim):
+            data = work[first:first + dim, :]
+            turned = jnp.concatenate([-data[:, lanes:], data[:, :lanes]], axis=1)
+            both = jnp.concatenate([data, turned], axis=0)
+            prod[first:first + dim, :] = jnp.dot(
+                bcat[...], both, preferred_element_type=jnp.float32
+            ).astype(jnp.bfloat16)
+
+    def swap_copy(round_no, step):
+        other = (me + step) % members
+        return pltpu.make_async_remote_copy(
+            src_ref=send.at[round_no, pl.ds(pl.multiple_of(other * piece, piece), piece)],
+            dst_ref=recv.at[round_no, pl.ds(pl.multiple_of(me * piece, piece), piece)],
+            send_sem=swap_send.at[round_no, step],
+            recv_sem=swap_recv.at[round_no, step],
+            device_id={"wide": other // 2, "narrow": other % 2},
+            device_id_type=MESH,
+        )
+
+    def swap_start(round_no):
+        for step in range(1, members):
+            launch(swap_copy(round_no, step))
+        mine = pl.ds(pl.multiple_of(me * piece, piece), piece)
+        recv[round_no, mine, :] = send[round_no, mine, :]
+
+    def swap_wait(round_no):
+        for step in range(1, members):
+            swap_copy(round_no, step).wait_recv()
+
+    line = lax.broadcasted_iota(jnp.int32, (1, total), 1)
+    send_own(0)
+    permute(stem_ref[...], work, gathered_place(0, line))
+    relay(0)
+    merge(0)
+    contract()
+    permute(prod[...], send.at[0], natural_place(0, line))
+    swap_start(0)
+    relay(1)
+    merge(1)
+    swap_wait(0)
+    permute(recv[0], work, gathered_place(1, line))
+    contract()
+    permute(prod[...], work, gathered_place(2, natural_place(1, line)))
+    relay(2)
+    merge(2)
+    contract()
+    permute(prod[...], send.at[1], natural_place(2, line))
+    swap_start(1)
+    swap_wait(1)
+    out_ref[0] = recv[1, :, :lanes].astype(jnp.float32)
+    out_ref[1] = recv[1, :, lanes:].astype(jnp.float32)
+    for copy in started:
+        copy.wait_send()
+
+
+def shards_in_kernel(stem_tensor, sub_branches, branch_bits):
+    count = lax.axis_size("wide")
+    wide_log = count.bit_length() - 1
+    lanes = 2**lane_bits
+    total = stem_tensor.shape[1] // lanes
+    bits = total.bit_length() - 1
+    dim = sub_branches.shape[-1]
+    half = count // 2
+    places = jnp.where(
+        branch_bits < LBITS,
+        branch_bits - lane_bits,
+        branch_bits - LBITS + bits - 1 - wide_log,
+    )
+    stem = (
+        stem_tensor.astype(jnp.bfloat16)
+        .reshape(2, total, lanes)
+        .transpose(1, 0, 2)
+        .reshape(total, 2 * lanes)
+    )
+    vmem = pl.BlockSpec(memory_space=pltpu.VMEM)
+    result = pl.pallas_call(
+        functools.partial(stem_kernel, count),
+        out_shape=jax.ShapeDtypeStruct((2, total, lanes), jnp.float32),
+        in_specs=[pl.BlockSpec(memory_space=pltpu.SMEM), vmem, vmem],
+        out_specs=vmem,
+        scratch_shapes=[
+            pltpu.VMEM((2, BRANCHES, 2, dim, dim), jnp.bfloat16),
+            pltpu.VMEM((dim, 2 * dim), jnp.bfloat16),
+            pltpu.VMEM((total, 2 * lanes), jnp.bfloat16),
+            pltpu.VMEM((total, 2 * lanes), jnp.bfloat16),
+            pltpu.VMEM((2, total, 2 * lanes), jnp.bfloat16),
+            pltpu.VMEM((2, total, 2 * lanes), jnp.bfloat16),
+            pltpu.SemaphoreType.DMA((BRANCHES, 2)),
+            pltpu.SemaphoreType.DMA((2, BRANCHES, 2, half)),
+            pltpu.SemaphoreType.DMA((2, BRANCHES, 2, half)),
+            pltpu.SemaphoreType.DMA((BRANCHES, 2, count)),
+            pltpu.SemaphoreType.DMA((BRANCHES, 2, count)),
+            pltpu.SemaphoreType.DMA((2, 2 * count)),
+            pltpu.SemaphoreType.DMA((2, 2 * count)),
+        ],
+        compiler_params=pltpu.CompilerParams(collective_id=0, has_side_effects=True),
+    )(places, stem, sub_branches[:, 0])
+    return result.reshape(2, -1)
+
+
+sublane_tile = 16
+
+
 def solution(mesh):
     in_specs = (P(None, ("cuts", "wide", "narrow")), P(None, "narrow", None, "wide", None), P())
     out_specs = P(None, ("cuts", "wide", "narrow"))
-    return jax.shard_map(shards, mesh=mesh, in_specs=in_specs, out_specs=out_specs, check_vma=False)
+
+    def run(stem_tensor, sub_branches, branch_bits):
+        whole_tiles = sub_branches.shape[3] % sublane_tile == 0
+        body = shards_in_kernel if whole_tiles else shards
+        return body(stem_tensor, sub_branches, branch_bits)
+
+    return jax.shard_map(run, mesh=mesh, in_specs=in_specs, out_specs=out_specs, check_vma=False)

time: 285 us -> 88.8 us (0.31)
  other arithmetic: 94.5 us -> 2.86 us
  Pallas kernels: 0 us -> 80.5 us
  waiting for transfers between devices: 60.5 us -> 0 us
  local copies, waits for them, and re-layouts: 58.5 us -> 3.88 us
  blocking collectives: 38.6 us -> 0 us
  between operations: 13.7 us -> 0.01 us
  matrix products: 13 us -> 0 us
  starting transfers between devices: 5.07 us -> 0 us
    pallas_call x0 -> x1, Pallas kernels: none -> 80.5 us  [shards_in_kernel(): pl.pallas_call(functools.partial(stem_kernel, count), out_shape=jax.Shape...]
    add x14 -> x0, other arithmetic: 72.9 us -> none  [the longest x3 37.2 us: bit_tables(): row_part = row_part + jnp.where(chosen[position], 0, bit_value)]
    all_to_all x3 -> x0, blocking collectives: 38.6 us -> none  [the longest x1 29.4 us: move_wide(): lax.all_to_all(amplitude.reshape(block_shape), 'wide', split_axis=1, conc...]
    all_gather x3 -> x0, waiting for transfers between devices: 38.2 us -> none  [shards(): own_whole = lax.all_gather(own_rows, 'wide', axis=1, tiled=True)]
    gather x9 -> x0, local copies, waits for them, and re-layouts: 30.7 us -> none  [the longest x6 16.1 us: contract_blocks(): picked = jnp.take(blocks, gather_index, axis=1)]
    all_to_all x1 -> x0, waiting for transfers between devices: 20.9 us -> none  [move_wide(): lax.all_to_all(amplitude.reshape(block_shape), 'wide', split_axis=1, conc...]
    select_n x11 -> x1, other arithmetic: 17.2 us -> 1.27 us  [shards_in_kernel(): jnp.where(branch_bits < LBITS, branch_bits - lane_bits, branch_bits - LBI...]
    dot_general x24 -> x0, matrix products: 13 us -> none  [the longest x12 7.8 us: real_product(): jnp.einsum('rul,cu->rcl', data, matrix, precision=lax.Precision.HIGHEST,...]
  transfers between devices with their start and end apart: 7 -> 0, of which waited for: 3 -> 0; matrix products, arithmetic and copies ran while one was open for 41% -> 0% of each run, Pallas kernels for 0% -> 0%
where the time goes in v1:
time: 88.8 us; the launch traced here: 87.2 us
  Pallas kernels  80.5 us (91%)
  local copies, waits for them, and re-layouts  3.88 us (4%)
  other arithmetic  2.86 us (3%)
    pallas_call x1, Pallas kernels, shards_in_kernel(): pl.pallas_call(functools.partial(stem_kernel, count), out_shape=jax.Shape...  80.5 us
    unnamed x2, local copies, waits for them, and re-layouts  3.88 us

profile of v1, /device:TPU:0, one launch (start us, length us, event | category | flops | bytes accessed | tf_op | source)
XLA Modules:
  0.0 87.2 jit_solution(12996875857629179302)
XLA Ops:
  0.0 1.3 %add_select_fusion.places_ref = s32[3,9]{1,0:T(4,128)} fusion(s32[3,9]{1,0:T(4,128)} %param.5), kind=kLoop, calls=%fused_computation.2 | loop fusion | flops 108 | bytes 216 | tf_op jit(solution)/shard_map/jit(_where)/select_n | solution.py:378
  1.3 1.6 %convert_element_type.3 = bf16[2,131072]{1,0:T(2,128)(2,1)S(1)} convert(f32[2,131072]{1,0:T(2,128)} %param.3) | non-fusion elementwise | flops 262144 | bytes 1572864 | tf_op jit(solution)/shard_map/convert_element_type | solution.py:384
  2.9 0.9 %copy.10 = bf16[128,8,2,128]{3,1,2,0:T(8,128)(2,1)} copy(bf16[128,8,2,128]{3,2,1,0:T(2,128)(2,1)S(1)} %bitcast.14) | data formatting | bytes 1048576
  3.7 80.5 %shard_map.37 = f32[2,1024,128]{2,1,0:T(8,128)} custom-call(s32[3,9]{1,0:T(4,128)} %add_select_fusion.places_ref, bf16[1024,256]{1,0:T(8,128)(2,1)} %bitcast.13, bf16[3,2,64,512]{3,2,1,0:T(8,128)(2,1)} %bitcast.15), custom_call_target="tpu_custom_call" | custom-call | tf_op jit(solution)/shard_map/pallas_call | solution.py:390
  84.2 3.0 %copy.9 = f32[1,2,1024,128]{3,1,2,0:T(2,128)} copy(f32[1,2,1024,128]{3,2,1,0:T(8,128)} %bitcast.12) | data formatting | bytes 2097152

commit v2 on v1

--- a/solution.py
+++ b/solution.py
@@ -151,115 +151,195 @@
 MESH = pl.DeviceIdType.MESH
 
 
-def ring_place(wide, count):
-    return wide // 2 + (wide % 2) * (count - 1 - 2 * (wide // 2))
-
-
-def ring_member(place, count):
-    back = place // (count // 2)
-    return 2 * place + back * (2 * (count - 1 - place) + 1 - 2 * place)
-
-
 def stem_kernel(
     count, places_ref, stem_ref, sub_ref, out_ref,
     gath, bcat, work, prod, send, recv,
-    own_sem, ring_send, ring_recv, pair_send, pair_recv, swap_send, swap_recv,
+    own_sem, z_send, z_recv, x_send, x_recv, y_send, y_recv,
+    pair_send, pair_recv, swap_send, swap_recv,
 ):
     wide = lax.axis_index("wide")
     narrow = lax.axis_index("narrow")
+    cut = lax.axis_index("cuts")
     rows = sub_ref.shape[2]
     branches = sub_ref.shape[0]
     dim = bcat.shape[0]
-    total = stem_ref.shape[0]
+    total = work.shape[0]
+    lanes = work.shape[1] // 2
     bits = total.bit_length() - 1
-    half = count // 2
-    lanes = stem_ref.shape[1] // 2
-    place = ring_place(wide, count)
-    neighbours = (
-        ring_member((place + 1) % count, count),
-        ring_member((place + count - 1) % count, count),
-    )
+    depth = count // 2
+    z = wide // 2
+    x = wide % 2
     members = 2 * count
     me = wide * 2 + narrow
     piece = total // members
 
     barrier = pltpu.get_barrier_semaphore()
-    for neighbour in neighbours:
-        pl.semaphore_signal(barrier, inc=1, device_id={"wide": neighbour}, device_id_type=MESH)
-    pl.semaphore_signal(barrier, inc=1, device_id={"narrow": 1 - narrow}, device_id_type=MESH)
-    pl.semaphore_wait(barrier, 3)
-
-    def block_rows(offset):
-        origin = ring_member((place + count - offset) % count, count)
-        return pl.ds(pl.multiple_of(origin * rows, rows), rows)
-
-    def used(way, part, distance):
-        return distance < half or (distance == half and part == way)
-
-    def offset_of(way, distance):
-        return distance if way == 0 else (count - distance) % count
+    for target in ({"wide": 2 * z + 1 - x}, {"cuts": 1 - cut}, {"narrow": 1 - narrow}):
+        pl.semaphore_signal(barrier, inc=1, device_id=target, device_id_type=MESH)
+
+    @pl.when(z + 1 < depth)
+    def _():
+        pl.semaphore_signal(barrier, inc=1, device_id={"wide": wide + 2}, device_id_type=MESH)
+
+    @pl.when(z > 0)
+    def _():
+        pl.semaphore_signal(barrier, inc=1, device_id={"wide": wide - 2}, device_id_type=MESH)
+
+    pl.semaphore_wait(barrier, 3 + jnp.minimum(z, 1) + jnp.minimum(depth - 1 - z, 1))
 
     started = []
-
-    def ring_copy(way, which, part, distance):
-        target = gath.at[narrow, which, part, block_rows(offset_of(way, distance - 1))]
+    own_copies = []
+
+    def there(way, distance):
+        return z >= distance if way == 0 else z + distance < depth
+
+    def level(way, distance):
+        return z - distance if way == 0 else z + distance
+
+    def slot_of(way, distance):
+        return 0 if distance == 0 else 1 + way * (depth - 1) + distance - 1
+
+    def part_of(side):
+        return cut if side == 0 else 1 - cut
+
+    def copy_of(which, side, column, way, distance, send_sem, recv_sem, device_id):
+        origin = 2 * level(way, distance) + (x if column == 0 else 1 - x)
+        span = pl.ds(pl.multiple_of(origin * rows, rows), rows)
+        target = gath.at[narrow, which, part_of(side), span]
+        own = distance == 0 and column == 0
         return pltpu.make_async_remote_copy(
-            src_ref=sub_ref.at[which, part] if distance == 1 else target,
+            src_ref=sub_ref.at[which, part_of(side)] if own else target,
             dst_ref=target,
-            send_sem=ring_send.at[way, which, part, distance - 1],
-            recv_sem=ring_recv.at[way, which, part, distance - 1],
-            device_id={"wide": neighbours[way]},
+            send_sem=send_sem,
+            recv_sem=recv_sem,
+            device_id=device_id,
             device_id_type=MESH,
         )
 
-    def pair_copy(which, part, offset):
-        target = gath.at[narrow, which, part, block_rows(offset)]
-        return pltpu.make_async_remote_copy(
-            src_ref=sub_ref.at[which, part] if offset == 0 else target,
-            dst_ref=target,
-            send_sem=pair_send.at[which, part, offset],
-            recv_sem=pair_recv.at[which, part, offset],
-            device_id={"narrow": 1 - narrow},
-            device_id_type=MESH,
-        )
-
-    def launch(copy):
-        copy.start()
-        started.append(copy)
-
-    own_copies = []
+    def z_copy(which, way, distance):
+        return copy_of(
+            which, 0, 0, way, distance - 1,
+            z_send.at[way, which, distance - 1], z_recv.at[way, which, distance - 1],
+            {"wide": wide + 2 if way == 0 else wide - 2},
+        )
+
+    def x_copy(which, side, way, distance):
+        slot = side if distance == 0 else 1 + slot_of(way, distance)
+        return copy_of(
+            which, side, 0, way, distance,
+            x_send.at[which, slot], x_recv.at[which, slot], {"wide": 2 * z + 1 - x},
+        )
+
+    def y_copy(which, column, way, distance):
+        slot = slot_of(way, distance)
+        return copy_of(
+            which, 0, column, way, distance,
+            y_send.at[which, column, slot], y_recv.at[which, column, slot],
+            {"cuts": 1 - cut},
+        )
+
+    def pair_copy(which, side, column, way, distance):
+        slot = slot_of(way, distance)
+        return copy_of(
+            which, side, column, way, distance,
+            pair_send.at[which, side, column, slot], pair_recv.at[which, side, column, slot],
+            {"narrow": 1 - narrow},
+        )
+
+    def launch(build, guard=None):
+        if guard is None:
+            build().start()
+        else:
+            pl.when(guard)(lambda: build().start())
+        started.append((build, guard))
+
+    def finish(build, guard):
+        if guard is None:
+            build().wait_send()
+        else:
+            pl.when(guard)(lambda: build().wait_send())
+
+    def await_recv(build, guard=None):
+        if guard is None:
+            build().wait_recv()
+        else:
+            pl.when(guard)(lambda: build().wait_recv())
+
+    ways = (0, 1)
+    part_sides = (0, 1)
+    call = functools.partial
 
     def send_own(which):
-        for part in range(2):
-            for way in range(2):
-                if used(way, part, 1):
-                    launch(ring_copy(way, which, part, 1))
-        for part in range(2):
-            launch(pair_copy(which, part, 0))
+        launch(call(z_copy, which, 0, 1), there(1, 1))
+        launch(call(z_copy, which, 1, 1), there(0, 1))
+        for side in part_sides:
+            launch(call(x_copy, which, side, 0, 0))
+        for side in part_sides:
+            launch(call(pair_copy, which, side, 0, 0, 0))
+            origin = pl.ds(pl.multiple_of(wide * rows, rows), rows)
             keep = pltpu.make_async_copy(
-                sub_ref.at[which, part],
-                gath.at[narrow, which, part, block_rows(0)],
-                own_sem.at[which, part],
+                sub_ref.at[which, side], gath.at[narrow, which, side, origin],
+                own_sem.at[which, side],
             )
             keep.start()
             own_copies.append(keep)
 
-    def relay(which):
-        for distance in range(1, half + 1):
-            for part in range(2):
-                for way in range(2):
-                    if not used(way, part, distance):
-                        continue
-                    ring_copy(way, which, part, distance).wait_recv()
-                    if used(way, part, distance + 1):
-                        launch(ring_copy(way, which, part, distance + 1))
-                    launch(pair_copy(which, part, offset_of(way, distance)))
-            if distance == max(half - 1, 1) and which + 1 < branches:
-                send_own(which + 1)
-        for part in range(2):
-            own_copies[2 * which + part].wait()
-            for offset in range(count):
-                pair_copy(which, part, offset).wait_recv()
+    def take_x_own(which):
+        for side in part_sides:
+            await_recv(call(x_copy, which, side, 0, 0))
+            launch(call(pair_copy, which, side, 1, 0, 0))
+
+    def take_z(which, distance):
+        for way in ways:
+            guard = there(way, distance)
+            await_recv(call(z_copy, which, way, distance), guard)
+            if distance + 1 < depth:
+                launch(
+                    call(z_copy, which, way, distance + 1),
+                    jnp.logical_and(guard, there(1 - way, 1)),
+                )
+            launch(call(y_copy, which, 0, way, distance), guard)
+            launch(call(x_copy, which, 0, way, distance), guard)
+            launch(call(pair_copy, which, 0, 0, way, distance), guard)
+
+    def take_x(which, distance):
+        for way in ways:
+            guard = there(way, distance)
+            await_recv(call(x_copy, which, 0, way, distance), guard)
+            launch(call(y_copy, which, 1, way, distance), guard)
+            launch(call(pair_copy, which, 0, 1, way, distance), guard)
+
+    def take_y(which, distance):
+        for way in ways:
+            guard = there(way, distance)
+            for column in (0, 1):
+                await_recv(call(y_copy, which, column, way, distance), guard)
+                launch(call(pair_copy, which, 1, column, way, distance), guard)
+
+    def complete(which):
+        for side in part_sides:
+            own_copies[2 * which + side].wait()
+            for column in (0, 1):
+                await_recv(call(pair_copy, which, side, column, 0, 0))
+                for way in ways:
+                    for distance in range(1, depth):
+                        await_recv(
+                            call(pair_copy, which, side, column, way, distance),
+                            there(way, distance),
+                        )
+
+    def relay(which, first, last):
+        if first == 1:
+            take_x_own(which)
+        for distance in range(first, last + 1):
+            if distance < depth:
+                take_z(which, distance)
+                take_x(which, distance)
+
+    def take_mates(which):
+        for distance in range(1, depth):
+            take_y(which, distance)
+        complete(which)
 
     def merge(which):
         first = [gath[0, which, part] for part in range(2)]
@@ -277,10 +357,18 @@
 
     width = dim.bit_length() - 1
 
+    narrow_place = bits - 1 - (count.bit_length() - 1)
+
+    def named_place(which, slot):
+        bit = places_ref[which, slot]
+        return bit + jnp.where(bit < LBITS, -lane_bits, narrow_place - LBITS)
+
+    places = [[named_place(which, slot) for slot in range(width)] for which in range(branches)]
+
     def free_place(which):
         rest = bits * (bits - 1) // 2
         for slot in range(width):
-            rest = rest - places_ref[which, slot]
+            rest = rest - places[which][slot]
         return rest
 
     def bit_at(values, position):
@@ -290,7 +378,7 @@
         found = jnp.left_shift(bit_at(values, free_place(which)), width)
         for slot in range(width):
             found = found + jnp.left_shift(
-                bit_at(values, places_ref[which, slot]), width - 1 - slot
+                bit_at(values, places[which][slot]), width - 1 - slot
             )
         return found
 
@@ -298,7 +386,7 @@
         found = jnp.left_shift(bit_at(values, width), free_place(which))
         for slot in range(width):
             found = found + jnp.left_shift(
-                bit_at(values, width - 1 - slot), places_ref[which, slot]
+                bit_at(values, width - 1 - slot), places[which][slot]
             )
         return found
 
@@ -331,65 +419,75 @@
             device_id_type=MESH,
         )
 
+    far_first = sorted(range(1, members), key=lambda step: -min(step, members - step))
+
     def swap_start(round_no):
-        for step in range(1, members):
-            launch(swap_copy(round_no, step))
+        for step in far_first:
+            launch(call(swap_copy, round_no, step))
         mine = pl.ds(pl.multiple_of(me * piece, piece), piece)
         recv[round_no, mine, :] = send[round_no, mine, :]
 
     def swap_wait(round_no):
-        for step in range(1, members):
+        for step in far_first:
             swap_copy(round_no, step).wait_recv()
 
     line = lax.broadcasted_iota(jnp.int32, (1, total), 1)
     send_own(0)
-    permute(stem_ref[...], work, gathered_place(0, line))
-    relay(0)
+    stem = jnp.concatenate(
+        [stem_ref[pl.ds(part, total, stride=2), :] for part in range(2)], axis=1
+    ).astype(jnp.bfloat16)
+    permute(stem, work, gathered_place(0, line))
+    middle = max(depth - 2, 1)
+    relay(0, 1, middle)
+    send_own(1)
+    relay(0, middle + 1, depth - 1)
+    relay(1, 1, 1)
+    take_mates(0)
     merge(0)
     contract()
+    relay(1, 2, middle)
     permute(prod[...], send.at[0], natural_place(0, line))
     swap_start(0)
-    relay(1)
+    send_own(2)
+    relay(1, middle + 1, depth - 1)
+    relay(2, 1, 1)
+    take_mates(1)
     merge(1)
+    relay(2, 2, depth - 1)
     swap_wait(0)
     permute(recv[0], work, gathered_place(1, line))
     contract()
     permute(prod[...], work, gathered_place(2, natural_place(1, line)))
-    relay(2)
+    take_mates(2)
     merge(2)
     contract()
     permute(prod[...], send.at[1], natural_place(2, line))
     swap_start(1)
     swap_wait(1)
-    out_ref[0] = recv[1, :, :lanes].astype(jnp.float32)
-    out_ref[1] = recv[1, :, lanes:].astype(jnp.float32)
-    for copy in started:
-        copy.wait_send()
+    for part in range(2):
+        out_ref[pl.ds(part, total, stride=2), :] = recv[
+            1, :, part * lanes:(part + 1) * lanes
+        ].astype(jnp.float32)
+    for build, guard in started:
+        finish(build, guard)
 
 
 def shards_in_kernel(stem_tensor, sub_branches, branch_bits):
     count = lax.axis_size("wide")
-    wide_log = count.bit_length() - 1
+    depth = count // 2
     lanes = 2**lane_bits
     total = stem_tensor.shape[1] // lanes
-    bits = total.bit_length() - 1
     dim = sub_branches.shape[-1]
-    half = count // 2
-    places = jnp.where(
-        branch_bits < LBITS,
-        branch_bits - lane_bits,
-        branch_bits - LBITS + bits - 1 - wide_log,
-    )
-    stem = (
-        stem_tensor.astype(jnp.bfloat16)
-        .reshape(2, total, lanes)
-        .transpose(1, 0, 2)
-        .reshape(total, 2 * lanes)
-    )
+    stem = stem_tensor.reshape(2, total, lanes).transpose(1, 0, 2).reshape(2 * total, lanes)
     vmem = pl.BlockSpec(memory_space=pltpu.VMEM)
+    slots = 2 * depth - 1
+    semaphores = [(BRANCHES, 2)]
+    for shape in ((2, BRANCHES, depth), (BRANCHES, slots + 1), (BRANCHES, 2, slots),
+                  (BRANCHES, 2, 2, slots), (2, 2 * count)):
+        semaphores += [shape, shape]
     result = pl.pallas_call(
         functools.partial(stem_kernel, count),
-        out_shape=jax.ShapeDtypeStruct((2, total, lanes), jnp.float32),
+        out_shape=jax.ShapeDtypeStruct((2 * total, lanes), jnp.float32),
         in_specs=[pl.BlockSpec(memory_space=pltpu.SMEM), vmem, vmem],
         out_specs=vmem,
         scratch_shapes=[
@@ -399,17 +497,10 @@
             pltpu.VMEM((total, 2 * lanes), jnp.bfloat16),
             pltpu.VMEM((2, total, 2 * lanes), jnp.bfloat16),
             pltpu.VMEM((2, total, 2 * lanes), jnp.bfloat16),
-            pltpu.SemaphoreType.DMA((BRANCHES, 2)),
-            pltpu.SemaphoreType.DMA((2, BRANCHES, 2, half)),
-            pltpu.SemaphoreType.DMA((2, BRANCHES, 2, half)),
-            pltpu.SemaphoreType.DMA((BRANCHES, 2, count)),
-            pltpu.SemaphoreType.DMA((BRANCHES, 2, count)),
-            pltpu.SemaphoreType.DMA((2, 2 * count)),
-            pltpu.SemaphoreType.DMA((2, 2 * count)),
-        ],
+        ] + [pltpu.SemaphoreType.DMA(shape) for shape in semaphores],
         compiler_params=pltpu.CompilerParams(collective_id=0, has_side_effects=True),
-    )(places, stem, sub_branches[:, 0])
-    return result.reshape(2, -1)
+    )(branch_bits, stem, sub_branches[:, 0])
+    return result.reshape(total, 2, lanes).transpose(1, 0, 2).reshape(2, -1)
 
 
 sublane_tile = 16
@@ -420,7 +511,7 @@
     out_specs = P(None, ("cuts", "wide", "narrow"))
 
     def run(stem_tensor, sub_branches, branch_bits):
-        whole_tiles = sub_branches.shape[3] % sublane_tile == 0
+        whole_tiles = sub_branches.shape[3] % sublane_tile == 0 and mesh.shape["cuts"] == 2
         body = shards_in_kernel if whole_tiles else shards
         return body(stem_tensor, sub_branches, branch_bits)
 

time: 88.8 us -> 86.8 us (0.977); the launches traced: 87.2 us -> 86.7 us
  Pallas kernels: 80.5 us -> 84.4 us
  other arithmetic: 2.86 us -> 0 us
  local copies, waits for them, and re-layouts: 3.88 us -> 2.26 us
    pallas_call x1, Pallas kernels: 80.5 us -> 84.4 us  [shards_in_kernel(): pl.pallas_call(functools.partial(stem_kernel, count), out_shape=jax.Shape...]
    unnamed x2 -> x1, local copies, waits for them, and re-layouts: 3.88 us -> 2.26 us
    convert_element_type x1 -> x0, other arithmetic: 1.58 us -> none  [shards_in_kernel(): stem_tensor.astype(jnp.bfloat16).reshape(2, total, lanes).transpose(1, 0, 2)]
    select_n x1 -> x0, other arithmetic: 1.27 us -> none  [shards_in_kernel(): jnp.where(branch_bits < LBITS, branch_bits - lane_bits, branch_bits - LBI...]
where the time goes in v2:
time: 86.8 us; the launch traced here: 86.7 us
  Pallas kernels  84.4 us (97%)
  local copies, waits for them, and re-layouts  2.26 us (3%)
    pallas_call x1, Pallas kernels, shards_in_kernel(): pl.pallas_call(functools.partial(stem_kernel, count), out_shape=jax.Shape...  84.4 us
    unnamed x1, local copies, waits for them, and re-layouts  2.26 us

profile of v2, /device:TPU:0, one launch (start us, length us, event | category | flops | bytes accessed | tf_op | source)
XLA Modules:
  0.0 86.7 jit_solution(1166472565392345764)
XLA Ops:
  0.0 84.4 %shard_map.37 = f32[2048,128]{1,0:T(8,128)} custom-call(s32[3,9]{1,0:T(4,128)} %places_ref.1, f32[2048,128]{1,0:T(8,128)} %bitcast.12, bf16[3,2,64,512]{3,2,1,0:T(8,128)(2,1)} %bitcast.13), custom_call_target="tpu_custom_call" | custom-call | tf_op jit(solution)/shard_map/pallas_call | solution.py:488
  84.4 2.3 %copy.7 = f32[2,131072]{1,0:T(2,128)} copy(f32[2,131072]{1,0:T(2,128)} %bitcast.11) | data formatting | bytes 2097152

commit v3 on v2

--- a/solution.py
+++ b/solution.py
@@ -153,8 +153,8 @@
 
 def stem_kernel(
     count, places_ref, stem_ref, sub_ref, out_ref,
-    gath, bcat, work, prod, send, recv,
-    own_sem, z_send, z_recv, x_send, x_recv, y_send, y_recv,
+    gath, bcat, work, prod, send, recv, stem_held,
+    stem_sem, own_sem, z_send, z_recv, x_send, x_recv, y_send, y_recv,
     pair_send, pair_recv, swap_send, swap_recv,
 ):
     wide = lax.axis_index("wide")
@@ -162,7 +162,7 @@
     cut = lax.axis_index("cuts")
     rows = sub_ref.shape[2]
     branches = sub_ref.shape[0]
-    dim = bcat.shape[0]
+    dim = bcat.shape[1]
     total = work.shape[0]
     lanes = work.shape[1] // 2
     bits = total.bit_length() - 1
@@ -173,6 +173,8 @@
     me = wide * 2 + narrow
     piece = total // members
 
+    stem_copy = pltpu.make_async_copy(stem_ref, stem_held, stem_sem)
+    stem_copy.start()
     barrier = pltpu.get_barrier_semaphore()
     for target in ({"wide": 2 * z + 1 - x}, {"cuts": 1 - cut}, {"narrow": 1 - narrow}):
         pl.semaphore_signal(barrier, inc=1, device_id=target, device_id_type=MESH)
@@ -269,9 +271,11 @@
     part_sides = (0, 1)
     call = functools.partial
 
-    def send_own(which):
+    def send_own_z(which):
         launch(call(z_copy, which, 0, 1), there(1, 1))
         launch(call(z_copy, which, 1, 1), there(0, 1))
+
+    def send_own_x(which):
         for side in part_sides:
             launch(call(x_copy, which, side, 0, 0))
         for side in part_sides:
@@ -328,13 +332,19 @@
                             there(way, distance),
                         )
 
-    def relay(which, first, last):
-        if first == 1:
-            take_x_own(which)
-        for distance in range(first, last + 1):
-            if distance < depth:
+    def advance(slot):
+        for which in range(branches):
+            distance = slot - which
+            if 1 <= distance < depth:
                 take_z(which, distance)
-                take_x(which, distance)
+            if 1 <= distance - 1 < depth:
+                take_x(which, distance - 1)
+            if distance == 2:
+                take_x_own(which)
+                if which + 1 < branches:
+                    send_own_x(which + 1)
+            if which == 0 and 1 <= distance - 2 < depth:
+                take_y(which, distance - 2)
 
     def take_mates(which):
         for distance in range(1, depth):
@@ -342,16 +352,17 @@
         complete(which)
 
     def merge(which):
+        held = bcat.at[which % 2]
         first = [gath[0, which, part] for part in range(2)]
         second = [gath[1, which, part] for part in range(2)]
 
         def half_product(left, right):
             return jnp.dot(left, right, preferred_element_type=jnp.float32)
 
-        bcat[:, :dim] = (
+        held[:, :dim] = (
             half_product(first[0], second[0]) - half_product(first[1], second[1])
         ).astype(jnp.bfloat16)
-        bcat[:, dim:] = (
+        held[:, dim:] = (
             half_product(first[0], second[1]) + half_product(first[1], second[0])
         ).astype(jnp.bfloat16)
 
@@ -399,13 +410,13 @@
                 onehot, source, preferred_element_type=jnp.float32
             ).astype(jnp.bfloat16)
 
-    def contract():
+    def contract(which):
         for first in range(0, total, dim):
             data = work[first:first + dim, :]
             turned = jnp.concatenate([-data[:, lanes:], data[:, :lanes]], axis=1)
             both = jnp.concatenate([data, turned], axis=0)
             prod[first:first + dim, :] = jnp.dot(
-                bcat[...], both, preferred_element_type=jnp.float32
+                bcat[which % 2], both, preferred_element_type=jnp.float32
             ).astype(jnp.bfloat16)
 
     def swap_copy(round_no, step):
@@ -432,35 +443,33 @@
             swap_copy(round_no, step).wait_recv()
 
     line = lax.broadcasted_iota(jnp.int32, (1, total), 1)
-    send_own(0)
+    send_own_z(0)
+    send_own_x(0)
+    for which in range(1, branches):
+        send_own_z(which)
+    stem_copy.wait()
     stem = jnp.concatenate(
-        [stem_ref[pl.ds(part, total, stride=2), :] for part in range(2)], axis=1
+        [stem_held[pl.ds(part, total, stride=2), :] for part in range(2)], axis=1
     ).astype(jnp.bfloat16)
     permute(stem, work, gathered_place(0, line))
-    middle = max(depth - 2, 1)
-    relay(0, 1, middle)
-    send_own(1)
-    relay(0, middle + 1, depth - 1)
-    relay(1, 1, 1)
-    take_mates(0)
+    for slot in range(1, depth + 2):
+        advance(slot)
+    complete(0)
     merge(0)
-    contract()
-    relay(1, 2, middle)
+    contract(0)
     permute(prod[...], send.at[0], natural_place(0, line))
     swap_start(0)
-    send_own(2)
-    relay(1, middle + 1, depth - 1)
-    relay(2, 1, 1)
+    for slot in range(depth + 2, depth + branches):
+        advance(slot)
     take_mates(1)
     merge(1)
-    relay(2, 2, depth - 1)
+    take_mates(2)
+    merge(2)
     swap_wait(0)
     permute(recv[0], work, gathered_place(1, line))
-    contract()
+    contract(1)
     permute(prod[...], work, gathered_place(2, natural_place(1, line)))
-    take_mates(2)
-    merge(2)
-    contract()
+    contract(2)
     permute(prod[...], send.at[1], natural_place(2, line))
     swap_start(1)
     swap_wait(1)
@@ -480,6 +489,7 @@
     dim = sub_branches.shape[-1]
     stem = stem_tensor.reshape(2, total, lanes).transpose(1, 0, 2).reshape(2 * total, lanes)
     vmem = pl.BlockSpec(memory_space=pltpu.VMEM)
+    hbm = pl.BlockSpec(memory_space=pl.ANY)
     slots = 2 * depth - 1
     semaphores = [(BRANCHES, 2)]
     for shape in ((2, BRANCHES, depth), (BRANCHES, slots + 1), (BRANCHES, 2, slots),
@@ -488,15 +498,17 @@
     result = pl.pallas_call(
         functools.partial(stem_kernel, count),
         out_shape=jax.ShapeDtypeStruct((2 * total, lanes), jnp.float32),
-        in_specs=[pl.BlockSpec(memory_space=pltpu.SMEM), vmem, vmem],
+        in_specs=[pl.BlockSpec(memory_space=pltpu.SMEM), hbm, hbm],
         out_specs=vmem,
         scratch_shapes=[
             pltpu.VMEM((2, BRANCHES, 2, dim, dim), jnp.bfloat16),
-            pltpu.VMEM((dim, 2 * dim), jnp.bfloat16),
+            pltpu.VMEM((2, dim, 2 * dim), jnp.bfloat16),
             pltpu.VMEM((total, 2 * lanes), jnp.bfloat16),
             pltpu.VMEM((total, 2 * lanes), jnp.bfloat16),
             pltpu.VMEM((2, total, 2 * lanes), jnp.bfloat16),
             pltpu.VMEM((2, total, 2 * lanes), jnp.bfloat16),
+            pltpu.VMEM((2 * total, lanes), jnp.float32),
+            pltpu.SemaphoreType.DMA(()),
         ] + [pltpu.SemaphoreType.DMA(shape) for shape in semaphores],
         compiler_params=pltpu.CompilerParams(collective_id=0, has_side_effects=True),
     )(branch_bits, stem, sub_branches[:, 0])

time: 86.8 us -> 65.7 us (0.76)
  Pallas kernels: 84.4 us -> 63.2 us
    pallas_call x1, Pallas kernels: 84.4 us -> 63.2 us  [shards_in_kernel(): pl.pallas_call(functools.partial(stem_kernel, count), out_shape=jax.Shape...]
where the time goes in v3:
time: 65.7 us; the launch traced here: 65.5 us
  Pallas kernels  63.2 us (96%)
  local copies, waits for them, and re-layouts  2.26 us (3%)
    pallas_call x1, Pallas kernels, shards_in_kernel(): pl.pallas_call(functools.partial(stem_kernel, count), out_shape=jax.Shape...  63.2 us
    unnamed x1, local copies, waits for them, and re-layouts  2.26 us

profile of v3, /device:TPU:0, one launch (start us, length us, event | category | flops | bytes accessed | tf_op | source)
XLA Modules:
  0.0 65.5 jit_solution(6058611414096701234)
XLA Ops:
  0.0 63.2 %shard_map.37 = f32[2048,128]{1,0:T(8,128)} custom-call(s32[3,9]{1,0:T(4,128)} %places_ref.1, f32[2048,128]{1,0:T(8,128)} %bitcast.12, bf16[3,2,64,512]{3,2,1,0:T(8,128)(2,1)} %bitcast.13), custom_call_target="tpu_custom_call" | custom-call | tf_op jit(solution)/shard_map/pallas_call | solution.py:498
  63.2 2.3 %copy.7 = f32[2,131072]{1,0:T(2,128)} copy(f32[2,131072]{1,0:T(2,128)} %bitcast.11) | data formatting | bytes 2097152

commit v4 on v3

--- a/solution.py
+++ b/solution.py
@@ -218,10 +218,11 @@
             device_id_type=MESH,
         )
 
-    def z_copy(which, way, distance):
+    def z_copy(which, side, way, distance):
+        slot = depth - 1 if side == 1 else distance - 1
         return copy_of(
-            which, 0, 0, way, distance - 1,
-            z_send.at[way, which, distance - 1], z_recv.at[way, which, distance - 1],
+            which, side, 0, way, distance - 1,
+            z_send.at[way, which, slot], z_recv.at[way, which, slot],
             {"wide": wide + 2 if way == 0 else wide - 2},
         )
 
@@ -272,8 +273,9 @@
     call = functools.partial
 
     def send_own_z(which):
-        launch(call(z_copy, which, 0, 1), there(1, 1))
-        launch(call(z_copy, which, 1, 1), there(0, 1))
+        for side in part_sides:
+            for way in ways:
+                launch(call(z_copy, which, side, way, 1), there(1 - way, 1))
 
     def send_own_x(which):
         for side in part_sides:
@@ -296,13 +298,14 @@
     def take_z(which, distance):
         for way in ways:
             guard = there(way, distance)
-            await_recv(call(z_copy, which, way, distance), guard)
+            await_recv(call(z_copy, which, 0, way, distance), guard)
             if distance + 1 < depth:
                 launch(
-                    call(z_copy, which, way, distance + 1),
+                    call(z_copy, which, 0, way, distance + 1),
                     jnp.logical_and(guard, there(1 - way, 1)),
                 )
-            launch(call(y_copy, which, 0, way, distance), guard)
+            if distance > 1:
+                launch(call(y_copy, which, 0, way, distance), guard)
             launch(call(x_copy, which, 0, way, distance), guard)
             launch(call(pair_copy, which, 0, 0, way, distance), guard)
 
@@ -317,7 +320,10 @@
         for way in ways:
             guard = there(way, distance)
             for column in (0, 1):
-                await_recv(call(y_copy, which, column, way, distance), guard)
+                if column == 0 and distance == 1:
+                    await_recv(call(z_copy, which, 1, way, 1), guard)
+                else:
+                    await_recv(call(y_copy, which, column, way, distance), guard)
                 launch(call(pair_copy, which, 1, column, way, distance), guard)
 
     def complete(which):
@@ -349,7 +355,6 @@
     def take_mates(which):
         for distance in range(1, depth):
             take_y(which, distance)
-        complete(which)
 
     def merge(which):
         held = bcat.at[which % 2]
@@ -419,28 +424,49 @@
                 bcat[which % 2], both, preferred_element_type=jnp.float32
             ).astype(jnp.bfloat16)
 
-    def swap_copy(round_no, step):
-        other = (me + step) % members
-        return pltpu.make_async_remote_copy(
-            src_ref=send.at[round_no, pl.ds(pl.multiple_of(other * piece, piece), piece)],
-            dst_ref=recv.at[round_no, pl.ds(pl.multiple_of(me * piece, piece), piece)],
-            send_sem=swap_send.at[round_no, step],
-            recv_sem=swap_recv.at[round_no, step],
-            device_id={"wide": other // 2, "narrow": other % 2},
-            device_id_type=MESH,
-        )
-
-    far_first = sorted(range(1, members), key=lambda step: -min(step, members - step))
-
-    def swap_start(round_no):
-        for step in far_first:
-            launch(call(swap_copy, round_no, step))
+    far_first = sorted(range(depth), key=lambda hop: -min(hop, depth - hop))
+    level_rows = total // depth
+
+    def swap_targets(round_no, hop):
+        level_z = (z + hop) % depth
+        for turn in range(4):
+            across, other_core = turn // 2, turn % 2
+            if hop == 0 and turn == 0:
+                continue
+            to_x = x if across == 0 else 1 - x
+            to_core = narrow if other_core == 0 else 1 - narrow
+            to_wide = 2 * level_z + to_x
+            other = 2 * to_wide + to_core
+            yield pltpu.make_async_remote_copy(
+                src_ref=send.at[round_no, pl.ds(pl.multiple_of(other * piece, piece), piece)],
+                dst_ref=recv.at[round_no, pl.ds(pl.multiple_of(me * piece, piece), piece)],
+                send_sem=swap_send.at[round_no, 4 * hop + turn],
+                recv_sem=swap_recv.at[round_no, 4 * hop + turn],
+                device_id={"wide": to_wide, "narrow": to_core},
+                device_id_type=MESH,
+            )
+
+    def swap_level(round_no, hop, source, goal):
+        first = ((z + hop) % depth) * level_rows
+        index = lax.broadcasted_iota(jnp.int32, (level_rows, total), 0) + first
+        onehot = (index == goal).astype(jnp.float32).astype(jnp.bfloat16)
+        send[round_no, pl.ds(pl.multiple_of(first, level_rows), level_rows), :] = jnp.dot(
+            onehot, source, preferred_element_type=jnp.float32
+        ).astype(jnp.bfloat16)
+        for copy in swap_targets(round_no, hop):
+            copy.start()
+
+    def swap_out(round_no, goal):
+        source = prod[...]
+        for hop in far_first:
+            swap_level(round_no, hop, source, goal)
         mine = pl.ds(pl.multiple_of(me * piece, piece), piece)
         recv[round_no, mine, :] = send[round_no, mine, :]
 
     def swap_wait(round_no):
-        for step in far_first:
-            swap_copy(round_no, step).wait_recv()
+        for hop in far_first:
+            for copy in swap_targets(round_no, hop):
+                copy.wait_recv()
 
     line = lax.broadcasted_iota(jnp.int32, (1, total), 1)
     send_own_z(0)
@@ -457,26 +483,30 @@
     complete(0)
     merge(0)
     contract(0)
-    permute(prod[...], send.at[0], natural_place(0, line))
-    swap_start(0)
+    swap_out(0, natural_place(0, line))
     for slot in range(depth + 2, depth + branches):
         advance(slot)
     take_mates(1)
+    complete(1)
     merge(1)
     take_mates(2)
-    merge(2)
     swap_wait(0)
     permute(recv[0], work, gathered_place(1, line))
     contract(1)
     permute(prod[...], work, gathered_place(2, natural_place(1, line)))
+    complete(2)
+    merge(2)
     contract(2)
-    permute(prod[...], send.at[1], natural_place(2, line))
-    swap_start(1)
+    swap_out(1, natural_place(2, line))
     swap_wait(1)
     for part in range(2):
         out_ref[pl.ds(part, total, stride=2), :] = recv[
             1, :, part * lanes:(part + 1) * lanes
         ].astype(jnp.float32)
+    for round_no in range(2):
+        for hop in range(depth):
+            for copy in swap_targets(round_no, hop):
+                copy.wait_send()
     for build, guard in started:
         finish(build, guard)
 

time: 65.7 us -> 70.5 us (1.073); the launches traced: 65.5 us -> 69.3 us
  Pallas kernels: 63.2 us -> 67.1 us
    pallas_call x1, Pallas kernels: 63.2 us -> 67.1 us  [shards_in_kernel(): pl.pallas_call(functools.partial(stem_kernel, count), out_shape=jax.Shape...]
where the time goes in v4:
time: 70.5 us; the launch traced here: 69.3 us
  Pallas kernels  67.1 us (95%)
  local copies, waits for them, and re-layouts  2.26 us (3%)
    pallas_call x1, Pallas kernels, shards_in_kernel(): pl.pallas_call(functools.partial(stem_kernel, count), out_shape=jax.Shape...  67.1 us
    unnamed x1, local copies, waits for them, and re-layouts  2.26 us

profile of v4, /device:TPU:0, one launch (start us, length us, event | category | flops | bytes accessed | tf_op | source)
XLA Modules:
  0.0 69.3 jit_solution(14381502664847182201)
XLA Ops:
  0.0 67.1 %shard_map.37 = f32[2048,128]{1,0:T(8,128)} custom-call(s32[3,9]{1,0:T(4,128)} %places_ref.1, f32[2048,128]{1,0:T(8,128)} %bitcast.12, bf16[3,2,64,512]{3,2,1,0:T(8,128)(2,1)} %bitcast.13), custom_call_target="tpu_custom_call" | custom-call | tf_op jit(solution)/shard_map/pallas_call | solution.py:528
  67.1 2.3 %copy.7 = f32[2,131072]{1,0:T(2,128)} copy(f32[2,131072]{1,0:T(2,128)} %bitcast.11) | data formatting | bytes 2097152

commit v5 on v4

--- a/solution.py
+++ b/solution.py
@@ -273,9 +273,8 @@
     call = functools.partial
 
     def send_own_z(which):
-        for side in part_sides:
-            for way in ways:
-                launch(call(z_copy, which, side, way, 1), there(1 - way, 1))
+        for way in ways:
+            launch(call(z_copy, which, 0, way, 1), there(1 - way, 1))
 
     def send_own_x(which):
         for side in part_sides:
@@ -304,8 +303,7 @@
                     call(z_copy, which, 0, way, distance + 1),
                     jnp.logical_and(guard, there(1 - way, 1)),
                 )
-            if distance > 1:
-                launch(call(y_copy, which, 0, way, distance), guard)
+            launch(call(y_copy, which, 0, way, distance), guard)
             launch(call(x_copy, which, 0, way, distance), guard)
             launch(call(pair_copy, which, 0, 0, way, distance), guard)
 
@@ -320,10 +318,7 @@
         for way in ways:
             guard = there(way, distance)
             for column in (0, 1):
-                if column == 0 and distance == 1:
-                    await_recv(call(z_copy, which, 1, way, 1), guard)
-                else:
-                    await_recv(call(y_copy, which, column, way, distance), guard)
+                await_recv(call(y_copy, which, column, way, distance), guard)
                 launch(call(pair_copy, which, 1, column, way, distance), guard)
 
     def complete(which):
@@ -343,6 +338,8 @@
             distance = slot - which
             if 1 <= distance < depth:
                 take_z(which, distance)
+            if distance == 1 and which + 1 < branches:
+                send_own_z(which + 1)
             if 1 <= distance - 1 < depth:
                 take_x(which, distance - 1)
             if distance == 2:
@@ -471,8 +468,6 @@
     line = lax.broadcasted_iota(jnp.int32, (1, total), 1)
     send_own_z(0)
     send_own_x(0)
-    for which in range(1, branches):
-        send_own_z(which)
     stem_copy.wait()
     stem = jnp.concatenate(
         [stem_held[pl.ds(part, total, stride=2), :] for part in range(2)], axis=1
@@ -490,12 +485,12 @@
     complete(1)
     merge(1)
     take_mates(2)
+    complete(2)
+    merge(2)
     swap_wait(0)
     permute(recv[0], work, gathered_place(1, line))
     contract(1)
     permute(prod[...], work, gathered_place(2, natural_place(1, line)))
-    complete(2)
-    merge(2)
     contract(2)
     swap_out(1, natural_place(2, line))
     swap_wait(1)

time: 70.5 us -> 63.5 us (0.901)
  Pallas kernels: 67.1 us -> 60.6 us
    pallas_call x1, Pallas kernels: 67.1 us -> 60.6 us  [shards_in_kernel(): pl.pallas_call(functools.partial(stem_kernel, count), out_shape=jax.Shape...]
where the time goes in v5:
time: 63.5 us; the launch traced here: 62.9 us
  Pallas kernels  60.6 us (95%)
  local copies, waits for them, and re-layouts  2.26 us (4%)
    pallas_call x1, Pallas kernels, shards_in_kernel(): pl.pallas_call(functools.partial(stem_kernel, count), out_shape=jax.Shape...  60.6 us
    unnamed x1, local copies, waits for them, and re-layouts  2.26 us

profile of v5, /device:TPU:0, one launch (start us, length us, event | category | flops | bytes accessed | tf_op | source)
XLA Modules:
  0.0 62.9 jit_solution(11138421894245121469)
XLA Ops:
  0.0 60.6 %shard_map.37 = f32[2048,128]{1,0:T(8,128)} custom-call(s32[3,9]{1,0:T(4,128)} %places_ref.1, f32[2048,128]{1,0:T(8,128)} %bitcast.12, bf16[3,2,64,512]{3,2,1,0:T(8,128)(2,1)} %bitcast.13), custom_call_target="tpu_custom_call" | custom-call | tf_op jit(solution)/shard_map/pallas_call | solution.py:523
  60.6 2.3 %copy.7 = f32[2,131072]{1,0:T(2,128)} copy(f32[2,131072]{1,0:T(2,128)} %bitcast.11) | data formatting | bytes 2097152
